TPU v7x, 32 devices: a whole 2x2x4 slice. The times are simulated.
32 devices in a mesh: dp: 16 (over z, y, x), tensor: 2 (over core).
Axes of the slice: x: 2, y: 2, z: 4, core: 2. Of those that a mesh axis runs over, the one named last changes fastest.
Arguments:
- grads: bfloat16 [16, 256, 3584], P('dp', None, 'tensor'), may hold values from -6 to 6
- residual: float32 [16, 256, 3584], P('dp', None, 'tensor'), may hold values from -4 to 4
- q_prev: float32 [3584, 64], P('tensor'), may hold values from -6 to 6
Outputs:
- q_next: float32 [3584, 64], P('tensor')
- basis: float32 [256, 64], replicated
- new_residual: float32 [16, 256, 3584], P('dp', None, 'tensor')
All inputs are finite; a program needn't handle non-finite values.
Results may differ from a plain program's by a relative error of at most 0.0003.
Values sent between devices are 32-bit elements; how exact they have to be, the bound alone decides.
A program may use at most 64 MiB of HBM per device.

v0:
```python
import jax
import jax.numpy as jnp
from jax import lax
from jax.sharding import PartitionSpec as P


def local(grads, residual, q_prev):
    high = lax.Precision.HIGHEST
    count = lax.axis_size("dp")
    merged = grads[0].astype(jnp.float32) + residual[0]
    partial_left = jnp.dot(merged, q_prev, precision=high)
    left = lax.psum(partial_left, ("dp", "tensor")) / count
    gram = jnp.dot(left.T, left, precision=high)
    lower = jnp.linalg.cholesky(gram)
    basis = jax.scipy.linalg.solve_triangular(lower, left.T, lower=True).T
    q_next = lax.psum(jnp.dot(merged.T, basis, precision=high), "dp") / count
    update = jnp.dot(basis, q_next.T, precision=high)
    new_residual = merged - update
    return (q_next, basis, new_residual[None])


def solution(mesh):
    in_specs = (P("dp", None, "tensor"), P("dp", None, "tensor"), P("tensor", None))
    out_specs = (P("tensor", None), P(), P("dp", None, "tensor"))
    return jax.shard_map(local, mesh=mesh, in_specs=in_specs, out_specs=out_specs, check_vma=False)
```

profile of v0, /device:TPU:0, one launch (start us, length us, event | category | flops | bytes accessed | tf_op | source)
XLA Modules:
  0.0 274.1 jit_solution(10268975559233325000)
XLA Ops:
  7.2 0.0 copy-start
  7.2 0.0 copy-start.1
  7.2 0.0 copy-start.2
  7.2 0.0 all-reduce.3.cloned.1.call-start
  7.2 0.9 copy-done
  8.2 4.2 %fusion.3 = f32[256,64]{0,1:T(8,128)} fusion(f32[1792,64]{0,1:T(8,128)S(1)} %copy-done, f32[1,256,1792]{2,1,0:T(8,128)} %param.4, bf16[1,256,1792]{2,1,0:T(8,128)(2,1)} %param.3), kind=kOutput, calls=%fused_computation.4 | convolution fusion | flops 353239040 | bytes 3276800 | tf_op jit(solution)/shard_map/dot_general | solution.py:11
  12.4 0.0 all-reduce.3.cloned.1.call-update
  12.4 0.0 all-reduce.5.cloned.1.call-start
  12.4 123.9 %all-reduce.3.cloned.1.call-done = f32[256,64]{0,1:T(8,128)} async-done(((f32[256,64]{0,1:T(8,128)}), f32[256,64]{0,1:T(8,128)}) %all-reduce.3.cloned.1.call-update) | async-done | bytes 65552 | tf_op jit(solution)/shard_map/psum | solution.py:12
  136.3 1.1 fusion.7
  137.4 0.1 copy.6
  137.5 5.8 %cholesky.16 = f32[64,64]{1,0:T(8,128)S(1)} custom-call(f32[64,64]{1,0:T(8,128)S(1)} %fusion.11), custom_call_target="Cholesky" | custom-call | tf_op jit(solution)/shard_map/jit(cholesky)/cholesky | solution.py:14
  143.4 0.6 compare_reduce_fusion
  144.0 0.7 fusion.9
  144.7 4.9 %custom-call.7 = f32[1,64,64]{1,2,0:T(8,128)S(1)} custom-call(f32[1,64,64]{2,1,0:T(8,128)S(1)} %fusion.9), custom_call_target="InvertDiagBlocksLowerTriangular" | custom-call | tf_op jit(solution)/shard_map/jit(_solve_triangular)/triangular_solve | solution.py:15
  149.6 1.1 fusion.5
  150.7 0.0 copy-done.1
  150.7 0.0 copy-start.4
  150.7 2.2 fusion.1
  152.9 0.0 all-reduce.5.cloned.1.call-update
  152.9 110.3 %all-reduce.5.cloned.1.call-done = f32[1792,64]{0,1:T(8,128)} async-done(((f32[1792,64]{0,1:T(8,128)}), f32[1792,64]{0,1:T(8,128)}) %all-reduce.5.cloned.1.call-update) | async-done | bytes 458768 | tf_op jit(solution)/shard_map/psum | solution.py:16
  263.3 1.0 broadcast_multiply_fusion
  264.3 0.0 copy-start.3
  264.3 2.9 %fusion = f32[1,256,1792]{2,1,0:T(8,128)} fusion(f32[64,256]{1,0:T(8,128)S(1)} %fusion.5, f32[1792,64]{0,1:T(8,128)S(1)} %broadcast_multiply_fusion, f32[1,256,1792]{2,1,0:T(8,128)S(1)} %copy-done.1, bf16[1,256,1792]{2,1,0:T(8,128)(2,1)S(1)} %copy-done.2), kind=kOutput, calls=%fused_computation.1 | convolution fusion | flops 353697792 | bytes 5111808 | tf_op jit(solution)/shard_map/dot_general | solution.py:17
  (5 shorter events, 0.0 us)
Async XLA Ops:
  7.2 1.0 copy-start
  7.2 143.5 %copy-start.1 = (f32[1,256,1792]{2,1,0:T(8,128)S(1)}, f32[1,256,1792]{2,1,0:T(8,128)}, u32[]{:S(2)}) copy-start(f32[1,256,1792]{2,1,0:T(8,128)} %param.4) | copy-start | bytes 5505028
  7.2 143.5 %copy-start.2 = (bf16[1,256,1792]{2,1,0:T(8,128)(2,1)S(1)}, bf16[1,256,1792]{2,1,0:T(8,128)(2,1)}, u32[]{:S(2)}) copy-start(bf16[1,256,1792]{2,1,0:T(8,128)(2,1)} %param.3) | copy-start | bytes 2752516
  7.2 129.1 %all-reduce.3.cloned.1.call-start = ((), (), s32[]{:S(2)}) async-start(), calls=%async_computation | async-start | bytes 131072 | tf_op jit(solution)/shard_map/psum | solution.py:12
  12.4 250.9 %all-reduce.5.cloned.1.call-start = ((), (), s32[]{:S(2)}) async-start(), calls=%async_computation.1 | async-start | bytes 917504 | tf_op jit(solution)/shard_map/psum | solution.py:16
  150.7 113.6 %copy-start.4 = (f32[64,256]{1,0:T(8,128)}, f32[64,256]{1,0:T(8,128)S(1)}, u32[]{:S(2)}) copy-start(f32[64,256]{1,0:T(8,128)S(1)} %fusion.5) | copy-start | bytes 196612
  264.3 2.9 %copy-start.3 = (f32[1792,64]{0,1:T(8,128)}, f32[1792,64]{0,1:T(8,128)S(1)}, u32[]{:S(2)}) copy-start(f32[1792,64]{0,1:T(8,128)S(1)} %broadcast_multiply_fusion) | copy-start | bytes 1376260
Sparse Core Ops, SparseCore 0:
  14.2 122.1 all-reduce.2
  153.1 110.1 all-reduce.4
where the time goes:
time: 274 us
  waiting for transfers between devices  234 us (85%)
  between operations  14.1 us (5%)
  other arithmetic  13.1 us (5%)
  matrix products  11.4 us (4%)
    psum x1, waiting for transfers between devices, local(): left = lax.psum(partial_left, ('dp', 'tensor')) / count  124 us
    psum x1, waiting for transfers between devices, local(): q_next = lax.psum(jnp.dot(merged.T, basis, precision=high), 'dp') / count  110 us
    another operation x3, other arithmetic, local(): lower = jnp.linalg.cholesky(gram)  6.52 us
    another operation x2, other arithmetic, local(): basis = jax.scipy.linalg.solve_triangular(lower, left.T, lower=True).T  5.55 us
  transfers between devices with their start and end apart: 2, of which 2 were waited for; matrix products, arithmetic and copies ran while one was open for 0% of the time, Pallas kernels for 0%

commit v1 on v0

--- a/solution.py
+++ b/solution.py
@@ -9,7 +9,7 @@
     count = lax.axis_size("dp")
     merged = grads[0].astype(jnp.float32) + residual[0]
     partial_left = jnp.dot(merged, q_prev, precision=high)
-    left = lax.psum(partial_left, ("dp", "tensor")) / count
+    left = jnp.sum(lax.all_gather(partial_left, ("dp", "tensor")), axis=0) / count
     gram = jnp.dot(left.T, left, precision=high)
     lower = jnp.linalg.cholesky(gram)
     basis = jax.scipy.linalg.solve_triangular(lower, left.T, lower=True).T

time: 274 us -> 207 us (0.76)
  waiting for transfers between devices: 234 us -> 166 us
    psum x1 -> x0, waiting for transfers between devices: 124 us -> none  [local(): left = lax.psum(partial_left, ('dp', 'tensor')) / count]
    all_gather x0 -> x1, waiting for transfers between devices: none -> 57.6 us  [local(): lax.all_gather(partial_left, ('dp', 'tensor'))]
where the time goes in v1:
time: 207 us
  waiting for transfers between devices  166 us (80%)
  between operations  14.1 us (7%)
  other arithmetic  13.3 us (6%)
  matrix products  9.69 us (5%)
  local copies, waits for them, and re-layouts  3.37 us (2%)
    psum x1, waiting for transfers between devices, local(): q_next = lax.psum(jnp.dot(merged.T, basis, precision=high), 'dp') / count  108 us
    all_gather x1, waiting for transfers between devices, local(): lax.all_gather(partial_left, ('dp', 'tensor'))  57.6 us
    another operation x3, other arithmetic, local(): lower = jnp.linalg.cholesky(gram)  6.52 us
    another operation x2, other arithmetic, local(): basis = jax.scipy.linalg.solve_triangular(lower, left.T, lower=True).T  5.55 us
    dot_general x1, matrix products, local(): partial_left = jnp.dot(merged, q_prev, precision=high)  4.17 us
  transfers between devices with their start and end apart: 2, of which 2 were waited for; matrix products, arithmetic and copies ran while one was open for 0% of the time, Pallas kernels for 0%

profile of v1, /device:TPU:0, one launch (start us, length us, event | category | flops | bytes accessed | tf_op | source)
XLA Modules:
  0.0 206.8 jit_solution(14840862912151061973)
XLA Ops:
  7.2 0.0 copy-start
  7.2 0.0 all-gather.3.cloned.1.call-start
  7.2 1.0 copy-done
  8.2 4.2 %fusion.3 = f32[256,64]{0,1:T(8,128)} fusion(f32[1792,64]{0,1:T(8,128)S(1)} %copy-done, f32[1,256,1792]{2,1,0:T(8,128)} %param.4, bf16[1,256,1792]{2,1,0:T(8,128)(2,1)} %param.3), kind=kOutput, calls=%fused_computation.5 | convolution fusion | flops 353239040 | bytes 3276800 | tf_op jit(solution)/shard_map/dot_general | solution.py:11
  12.4 0.0 all-gather.3.cloned.1.call-update
  12.4 0.0 all-reduce.2.cloned.1.call-start
  12.4 57.6 %all-gather.3.cloned.1.call-done = f32[8192,64]{0,1:T(8,128)} async-done(((f32[256,64]{0,1:T(8,128)}), f32[8192,64]{0,1:T(8,128)}) %all-gather.3.cloned.1.call-update) | async-done | bytes 2097168 | tf_op jit(solution)/shard_map/all_gather | solution.py:12
  70.1 2.3 %copy.8 = f32[8,8,32,256]{3,2,1,0:T(8,128)S(1)} copy(f32[8,8,32,256]{3,1,2,0:T(8,128)} %bitcast.27) | data formatting | bytes 4194304
  72.4 0.0 copy-start.1
  72.4 0.2 bitcast_reduce_fusion
  72.6 0.2 fusion.7
  72.8 0.1 copy.7
  72.9 5.8 %cholesky.16 = f32[64,64]{1,0:T(8,128)S(1)} custom-call(f32[64,64]{1,0:T(8,128)S(1)} %fusion.11), custom_call_target="Cholesky" | custom-call | tf_op jit(solution)/shard_map/jit(cholesky)/cholesky | solution.py:14
  78.8 0.6 compare_reduce_fusion
  79.5 0.7 fusion.9
  80.1 4.9 %custom-call.7 = f32[1,64,64]{1,2,0:T(8,128)S(1)} custom-call(f32[1,64,64]{2,1,0:T(8,128)S(1)} %fusion.9), custom_call_target="InvertDiagBlocksLowerTriangular" | custom-call | tf_op jit(solution)/shard_map/jit(_solve_triangular)/triangular_solve | solution.py:15
  85.0 0.3 fusion.5
  85.3 0.0 copy-start.4
  85.3 2.2 %fusion.1 = f32[1792,64]{0,1:T(8,128)} fusion(f32[64,256]{1,0:T(8,128)S(1)} %fusion.5, f32[1,256,1792]{2,1,0:T(8,128)S(1)} %copy-done.1, bf16[1,256,1792]{2,1,0:T(8,128)(2,1)S(1)} %copy-done.2), kind=kOutput, calls=%fused_computation.3 | convolution fusion | flops 353239040 | bytes 3276800 | tf_op jit(solution)/shard_map/dot_general | solution.py:16
  87.5 0.0 all-reduce.2.cloned.1.call-update
  87.5 108.5 %all-reduce.2.cloned.1.call-done = f32[1792,64]{0,1:T(8,128)} async-done(((f32[1792,64]{0,1:T(8,128)}), f32[1792,64]{0,1:T(8,128)}) %all-reduce.2.cloned.1.call-update) | async-done | bytes 458768 | tf_op jit(solution)/shard_map/psum | solution.py:16
  196.0 1.0 broadcast_multiply_fusion
  197.1 0.0 copy-start.3
  197.1 2.9 %fusion = f32[1,256,1792]{2,1,0:T(8,128)} fusion(f32[64,256]{1,0:T(8,128)S(1)} %fusion.5, f32[1792,64]{0,1:T(8,128)S(1)} %broadcast_multiply_fusion, f32[1,256,1792]{2,1,0:T(8,128)S(1)} %copy-done.1, bf16[1,256,1792]{2,1,0:T(8,128)(2,1)S(1)} %copy-done.2), kind=kOutput, calls=%fused_computation.1 | convolution fusion | flops 353697792 | bytes 5111808 | tf_op jit(solution)/shard_map/dot_general | solution.py:17
  (7 shorter events, 0.0 us)
Async XLA Ops:
  7.2 1.0 copy-start
  7.2 62.9 %all-gather.3.cloned.1.call-start = ((), (), s32[]{:S(2)}) async-start(), calls=%async_computation.1 | async-start | bytes 2162688 | tf_op jit(solution)/shard_map/all_gather | solution.py:12
  12.4 183.6 %all-reduce.2.cloned.1.call-start = ((), (), s32[]{:S(2)}) async-start(), calls=%async_computation | async-start | bytes 917504 | tf_op jit(solution)/shard_map/psum | solution.py:16
  70.1 15.2 %copy-start.2 = (bf16[1,256,1792]{2,1,0:T(8,128)(2,1)S(1)}, bf16[1,256,1792]{2,1,0:T(8,128)(2,1)}, u32[]{:S(2)}) copy-start(bf16[1,256,1792]{2,1,0:T(8,128)(2,1)} %param.3) | copy-start | bytes 2752516
  72.4 12.9 %copy-start.1 = (f32[1,256,1792]{2,1,0:T(8,128)S(1)}, f32[1,256,1792]{2,1,0:T(8,128)}, u32[]{:S(2)}) copy-start(f32[1,256,1792]{2,1,0:T(8,128)} %param.4) | copy-start | bytes 5505028
  85.3 111.7 %copy-start.4 = (f32[64,256]{1,0:T(8,128)}, f32[64,256]{1,0:T(8,128)S(1)}, u32[]{:S(2)}) copy-start(f32[64,256]{1,0:T(8,128)S(1)} %fusion.5) | copy-start | bytes 196612
  197.1 2.9 %copy-start.3 = (f32[1792,64]{0,1:T(8,128)}, f32[1792,64]{0,1:T(8,128)S(1)}, u32[]{:S(2)}) copy-start(f32[1792,64]{0,1:T(8,128)S(1)} %broadcast_multiply_fusion) | copy-start | bytes 1376260
Sparse Core Ops, SparseCore 0:
  12.5 57.5 all-gather.2
  87.6 108.3 all-reduce.1
